TPU v7x, 256 devices: a whole 4x4x8 slice. The times are simulated.
256 devices in a mesh: dp: 16 (over y, x), key: 4 (over z_hi), tensor: 4 (over z_lo, core).
Axes of the slice: x: 4, y: 4, z: 8 (z_hi: 4, z_lo: 2; z = z_hi * 2 + z_lo), core: 2. Of those that a mesh axis runs over, the one named last changes fastest.
Arguments:
- queries: bfloat16 [16384, 8, 2, 256], P(('dp', 'key'), 'tensor'), may hold values from -6 to 6
- sub_keys: bfloat16 [1024, 8, 2, 256], P('key', 'tensor'), may hold values from -6 to 6
- query_weight: bfloat16 [4096, 4096], P(None, 'tensor'), may hold values from -0.09375 to 0.09375
- sub_choice: int32 [16384, 8, 2, 32], P(('dp', 'key'), 'tensor'), may hold values from 0 to 1023, all different within a row
- pair_choice: int32 [16384, 8, 32], P(('dp', 'key'), 'tensor'), may hold values from 0 to 1023, all different within a row
- weights: float32 [16384, 8, 32], P(('dp', 'key'), 'tensor'), may hold values from 0 to 1, as said below
- weight_grad: float32 [16384, 8, 32], P(('dp', 'key'), 'tensor'), may hold values from -6 to 6
Outputs:
- sub_key_grad: float32 [1024, 8, 2, 256], P(('dp', 'key'), 'tensor')
- input_grad: bfloat16 [16384, 4096], P(('dp', 'key', 'tensor'))
Inputs may be any that keep to these rules, and one draw needn't show every extreme that they name: Each row of weights is positive and sums to one.
All inputs are finite; a program needn't handle non-finite values.
Results may differ from a plain program's by a relative error of at most 0.0058.
Values may be sent and summed in bfloat16 or wider, within the bound.
A program may use at most 64 MiB of HBM per device.

v0:
```python
import math

import jax
import jax.numpy as jnp
from jax import lax
from jax.sharding import Mesh
from jax.sharding import PartitionSpec as P

DP = ("dp_0", "dp_1")
DP_KEY = ("dp_0", "dp_1", "key")
DP_KEY_TENSOR = ("dp_0", "dp_1", "key", "tensor")


def copy_for_each(x, axis):
    copies = jnp.broadcast_to(x, (lax.axis_size(axis), *x.shape))
    return lax.all_to_all(copies, axis, split_axis=0, concat_axis=0, tiled=True)


def laid_out(tiles, dim):
    shape = list(tiles.shape[1:])
    shape[dim] *= tiles.shape[0]
    return jnp.moveaxis(tiles, 0, dim).reshape(shape)


def gather_directly(x, axis, dim):
    tiles = copy_for_each(x, axis)
    return laid_out(tiles, dim)


def summed_rows(total, axes):
    for axis in axes:
        total = lax.psum_scatter(total, axis, scatter_dimension=0, tiled=True)
    return total


def in_blocks(x, dim, devices):
    before, after = (x.shape[:dim], x.shape[dim + 1 :])
    return jnp.moveaxis(x.reshape(*before, devices, -1, *after), dim, 0)


def sum_at_owner(x, axis, dim):
    devices = lax.axis_size(axis)
    tiles = lax.all_to_all(in_blocks(x, dim, devices), axis, 0, 0, tiled=True)
    return jnp.sum(tiles, axis=0)


def on_device(queries, sub_keys, query_weight, sub_choice, pair_choice, weights, weight_grad):
    tok, heads_here, halves, width = queries.shape
    topk = pair_choice.shape[2]
    nsub = sub_keys.shape[0] * lax.axis_size("key")
    score_grad = weights * (weight_grad - jnp.sum(weights * weight_grad, axis=-1, keepdims=True))
    slots = jnp.arange(topk, dtype=jnp.int32)
    first = pair_choice // topk
    second = pair_choice % topk
    grad_one = jnp.sum(
        score_grad[..., None] * (first[..., None] == slots).astype(jnp.float32), axis=2
    )
    grad_two = jnp.sum(
        score_grad[..., None] * (second[..., None] == slots).astype(jnp.float32), axis=2
    )
    slot_grad = jnp.stack([grad_one, grad_two], axis=2)
    count = tok * heads_here * halves
    lines_blk = math.gcd(count, 128)
    line_blocks = count // lines_blk
    row_ids = jnp.arange(nsub, dtype=jnp.int32)
    idx_blocks = sub_choice.reshape(line_blocks, lines_blk, topk)
    val_blocks = slot_grad.reshape(line_blocks, lines_blk, topk)

    def build_rows(pieces):
        idx_here, val_here = pieces
        match = idx_here[:, :, None] == row_ids[None, None, :]
        return jnp.sum(jnp.where(match, val_here[:, :, None], 0.0), axis=1).astype(jnp.bfloat16)

    table = lax.map(build_rows, (idx_blocks, val_blocks)).reshape(tok, heads_here, halves, nsub)
    part_rows = table
    query_grad = jnp.einsum(
        "thxr,rhxf->thxf",
        part_rows,
        gather_directly(sub_keys, "key", 0),
        preferred_element_type=jnp.float32,
    ).astype(jnp.bfloat16)
    part_rows = table
    partial_value = summed_rows(
        jnp.einsum("thxr,thxf->rhxf", part_rows, queries, preferred_element_type=jnp.float32), DP
    )
    sub_key_grad = sum_at_owner(partial_value, "key", 0)
    flat = query_grad.reshape(tok, heads_here * halves * width)
    part_rows = flat
    input_grad = sum_at_owner(
        lax.dot_general(
            part_rows, query_weight, (((1,), (1,)), ((), ())), preferred_element_type=jnp.float32
        ),
        "tensor",
        0,
    )
    return (sub_key_grad, input_grad.astype(jnp.bfloat16))


def solution(mesh):
    split = Mesh(
        mesh.devices.reshape(4, 4, mesh.shape["key"], mesh.shape["tensor"]),
        ("dp_0", "dp_1", "key", "tensor"),
    )
    in_specs = (
        P(DP_KEY, "tensor", None, None),
        P("key", "tensor", None, None),
        P(None, "tensor"),
        P(DP_KEY, "tensor", None, None),
        P(DP_KEY, "tensor", None),
        P(DP_KEY, "tensor", None),
        P(DP_KEY, "tensor", None),
    )
    out_specs = (P(DP_KEY, "tensor", None, None), P(DP_KEY_TENSOR, None))
    return jax.shard_map(
        on_device, mesh=split, in_specs=in_specs, out_specs=out_specs, check_vma=False
    )
```

profile of v0, /device:TPU:1, one launch (start us, length us, event | category | flops | bytes accessed | tf_op | source)
XLA Modules:
  0.0 175.4 jit_solution(2334793718907471379)
XLA Ops:
  7.2 0.0 copy-start
  7.2 1.2 copy.72
  8.4 1.6 broadcast_in_dim.24
  9.9 0.0 copy-start.3
  9.9 0.0 copy-start.4
  9.9 9.1 %all-to-all-start.1 = ((bf16[4,256,2,2,256]{4,1,3,2,0:T(8,128)(2,1)}), bf16[4,256,2,2,256]{4,1,3,2,0:T(8,128)(2,1)S(1)}, u32[]{:S(2)}, u32[]{:S(2)}) async-start(bf16[4,256,2,2,256]{4,1,3,2,0:T(8,128)(2,1)} %broadcast_in_dim.24), calls=%async_computation.3 | async-start | bytes 4194304 | tf_op jit(solution)/shard_map/all_to_all | solution.py:16
  19.1 0.0 reduce-scatter.3.cloned.1.call-start
  19.1 0.0 copy-done.3
  19.1 0.1 add_select_fusion
  19.1 0.0 copy-done.4
  19.2 0.0 copy-done.5
  19.2 0.1 subtract_multiply_fusion
  19.3 0.6 select_reduce_fusion.2
  20.0 0.3 copy.67
  20.3 0.0 copy-done.2
  20.3 1.0 copy.66
  21.3 42.3 %while.11 = (s32[]{:T(128)}, bf16[8,128,1024]{2,1,0:T(8,128)(2,1)}, s32[8,128,32]{2,1,0:T(8,128)}, f32[8,128,32]{2,1,0:T(8,128)S(1)}, s32[]{:T(128)}) while((s32[]{:T(128)}, bf16[8,128,1024]{2,1,0:T(8,128)(2,1)}, s32[8,128,32]{2,1,0:T(8,128)}, f32[8,128,32]{2,1,0:T(8,128)S(1)}, s32[]{:T(128)}) %tuple.39), condition=%wide.region_5.6_spmd.clone, body=%wide.region_3.5_spmd.clone.sunk | while | flops 12451842 | bytes 884817 | solution.py:74
  21.3 0.8 dynamic-slice_bitcast_fusion.5
  22.1 3.7 %select_reduce_fusion.4 = bf16[128,1024]{1,0:T(8,128)(2,1)S(1)} fusion(f32[128,32]{1,0:T(8,128)S(1)} %dynamic-slice_bitcast_fusion.4, s32[128,32]{1,0:T(8,128)S(1)} %dynamic-slice_bitcast_fusion.5), kind=kLoop, calls=%fused_computation.2.clone.1 | loop fusion | flops 12451840 | bytes 294912 | tf_op jit(solution)/shard_map/while/body/eval_jaxpr/reduce_sum | solution.py:72
  25.8 0.7 bitcast_dynamic-update-slice_fusion.2
  26.6 0.8 dynamic-slice_bitcast_fusion.5
  27.4 3.7 %select_reduce_fusion.4 = bf16[128,1024]{1,0:T(8,128)(2,1)S(1)} fusion(f32[128,32]{1,0:T(8,128)S(1)} %dynamic-slice_bitcast_fusion.4, s32[128,32]{1,0:T(8,128)S(1)} %dynamic-slice_bitcast_fusion.5), kind=kLoop, calls=%fused_computation.2.clone.1 | loop fusion | flops 12451840 | bytes 294912 | tf_op jit(solution)/shard_map/while/body/eval_jaxpr/reduce_sum | solution.py:72
  31.1 0.7 bitcast_dynamic-update-slice_fusion.2
  31.8 0.8 dynamic-slice_bitcast_fusion.5
  32.7 3.7 %select_reduce_fusion.4 = bf16[128,1024]{1,0:T(8,128)(2,1)S(1)} fusion(f32[128,32]{1,0:T(8,128)S(1)} %dynamic-slice_bitcast_fusion.4, s32[128,32]{1,0:T(8,128)S(1)} %dynamic-slice_bitcast_fusion.5), kind=kLoop, calls=%fused_computation.2.clone.1 | loop fusion | flops 12451840 | bytes 294912 | tf_op jit(solution)/shard_map/while/body/eval_jaxpr/reduce_sum | solution.py:72
  36.4 0.7 bitcast_dynamic-update-slice_fusion.2
  37.1 0.8 dynamic-slice_bitcast_fusion.5
  38.0 3.7 %select_reduce_fusion.4 = bf16[128,1024]{1,0:T(8,128)(2,1)S(1)} fusion(f32[128,32]{1,0:T(8,128)S(1)} %dynamic-slice_bitcast_fusion.4, s32[128,32]{1,0:T(8,128)S(1)} %dynamic-slice_bitcast_fusion.5), kind=kLoop, calls=%fused_computation.2.clone.1 | loop fusion | flops 12451840 | bytes 294912 | tf_op jit(solution)/shard_map/while/body/eval_jaxpr/reduce_sum | solution.py:72
  41.7 0.7 bitcast_dynamic-update-slice_fusion.2
  42.4 0.8 dynamic-slice_bitcast_fusion.5
  43.3 3.7 %select_reduce_fusion.4 = bf16[128,1024]{1,0:T(8,128)(2,1)S(1)} fusion(f32[128,32]{1,0:T(8,128)S(1)} %dynamic-slice_bitcast_fusion.4, s32[128,32]{1,0:T(8,128)S(1)} %dynamic-slice_bitcast_fusion.5), kind=kLoop, calls=%fused_computation.2.clone.1 | loop fusion | flops 12451840 | bytes 294912 | tf_op jit(solution)/shard_map/while/body/eval_jaxpr/reduce_sum | solution.py:72
  47.0 0.7 bitcast_dynamic-update-slice_fusion.2
  47.7 0.8 dynamic-slice_bitcast_fusion.5
  48.6 3.7 %select_reduce_fusion.4 = bf16[128,1024]{1,0:T(8,128)(2,1)S(1)} fusion(f32[128,32]{1,0:T(8,128)S(1)} %dynamic-slice_bitcast_fusion.4, s32[128,32]{1,0:T(8,128)S(1)} %dynamic-slice_bitcast_fusion.5), kind=kLoop, calls=%fused_computation.2.clone.1 | loop fusion | flops 12451840 | bytes 294912 | tf_op jit(solution)/shard_map/while/body/eval_jaxpr/reduce_sum | solution.py:72
  52.3 0.7 bitcast_dynamic-update-slice_fusion.2
  53.0 0.8 dynamic-slice_bitcast_fusion.5
  53.9 3.7 %select_reduce_fusion.4 = bf16[128,1024]{1,0:T(8,128)(2,1)S(1)} fusion(f32[128,32]{1,0:T(8,128)S(1)} %dynamic-slice_bitcast_fusion.4, s32[128,32]{1,0:T(8,128)S(1)} %dynamic-slice_bitcast_fusion.5), kind=kLoop, calls=%fused_computation.2.clone.1 | loop fusion | flops 12451840 | bytes 294912 | tf_op jit(solution)/shard_map/while/body/eval_jaxpr/reduce_sum | solution.py:72
  57.6 0.7 bitcast_dynamic-update-slice_fusion.2
  58.3 0.8 dynamic-slice_bitcast_fusion.5
  59.2 3.7 %select_reduce_fusion.4 = bf16[128,1024]{1,0:T(8,128)(2,1)S(1)} fusion(f32[128,32]{1,0:T(8,128)S(1)} %dynamic-slice_bitcast_fusion.4, s32[128,32]{1,0:T(8,128)S(1)} %dynamic-slice_bitcast_fusion.5), kind=kLoop, calls=%fused_computation.2.clone.1 | loop fusion | flops 12451840 | bytes 294912 | tf_op jit(solution)/shard_map/while/body/eval_jaxpr/reduce_sum | solution.py:72
  62.9 0.7 bitcast_dynamic-update-slice_fusion.2
  63.6 4.1 %reshape.42 = bf16[256,2,2,1024]{3,2,1,0:T(2,128)(2,1)} reshape(bf16[8,128,1024]{2,1,0:T(8,128)(2,1)} %get-tuple-element.29) | data formatting | bytes 4194304 | tf_op jit(solution)/shard_map/reshape | solution.py:74
  67.7 0.0 copy-done
  67.7 5.1 %convolution_bitcast_fusion = f32[1024,2,2,256]{3,0,2,1:T(8,128)} fusion(bf16[256,2,2,1024]{3,2,1,0:T(2,128)(2,1)} %reshape.42, bf16[256,2,2,256]{3,2,1,0:T(2,128)(2,1)S(1)} %copy-done), kind=kOutput, calls=%fused_computation.8 | convolution fusion | flops 536870912 | bytes 6815744 | tf_op jit(solution)/shard_map/thxr,thxf->rhxf/dot_general | solution.py:84
  72.8 0.0 reduce-scatter.3.cloned.1.call-update
  72.8 0.0 all-to-all-done.1
  72.8 0.0 copy-start.1
  72.8 0.1 copy.73
  73.0 1.4 copy-done.1
  74.4 0.8 fusion.10
  75.2 0.5 copy.75
  75.8 0.4 dot_general.13
  76.2 7.7 %fusion.2 = f32[4,64,4096]{2,1,0:T(8,128)} fusion(bf16[4,64,1024]{2,1,0:T(8,128)(2,1)S(1)} %dot_general.13, bf16[4096,1024]{1,0:T(8,128)(2,1)} %param.11), kind=kOutput, calls=%fused_computation.6 | convolution fusion | flops 2147483648 | bytes 13107200 | tf_op jit(solution)/shard_map/dot_general | solution.py:90
  83.9 6.1 %all-to-all-start.2 = ((f32[4,64,4096]{2,1,0:T(8,128)}), f32[4,64,4096]{2,1,0:T(8,128)}, u32[]{:S(2)}, u32[]{:S(2)}) async-start(f32[4,64,4096]{2,1,0:T(8,128)} %fusion.2), calls=%async_computation.4 | async-start | bytes 8388608 | tf_op jit(solution)/shard_map/all_to_all | solution.py:43
  90.0 0.0 reduce-scatter.5.cloned.1.call-start
  90.0 34.4 %reduce-scatter.3.cloned.1.call-done = f32[256,2,2,256]{3,0,2,1:T(8,128)} async-done(((f32[1024,2,2,256]{3,0,2,1:T(8,128)}), f32[256,2,2,256]{3,0,2,1:T(8,128)}) %reduce-scatter.3.cloned.1.call-update) | async-done | bytes 1048592 | tf_op jit(solution)/shard_map/reduce_scatter | solution.py:32
  124.3 0.0 reduce-scatter.5.cloned.1.call-update
  124.3 27.1 %reduce-scatter.5.cloned.1.call-done = f32[64,2,2,256]{3,0,2,1:T(8,128)} async-done(((f32[256,2,2,256]{3,0,2,1:T(8,128)}), f32[64,2,2,256]{3,0,2,1:T(8,128)}) %reduce-scatter.5.cloned.1.call-update) | async-done | bytes 262160 | tf_op jit(solution)/shard_map/reduce_scatter | solution.py:32
  151.4 1.7 copy.70
  153.1 0.0 all-to-all-done.2
  153.1 6.8 %all-to-all-start = ((f32[4,16,2,2,256]{4,1,3,2,0:T(8,128)}), f32[4,16,2,2,256]{4,1,3,2,0:T(8,128)S(1)}, u32[]{:S(2)}, u32[]{:S(2)}) async-start(f32[4,16,2,2,256]{4,1,3,2,0:T(8,128)} %copy.70), calls=%async_computation.2 | async-start | bytes 524288 | tf_op jit(solution)/shard_map/all_to_all | solution.py:43
  159.9 3.4 %reduce_sum.58 = bf16[64,4096]{1,0:T(8,128)(2,1)} reduce(f32[4,64,4096]{2,1,0:T(8,128)} %all-to-all-done.2, f32[]{:T(128)} %constant.46.clone.1), dimensions={0}, to_apply=%region_9.10 | reduce | flops 786432 | bytes 4718596 | tf_op jit(solution)/shard_map/reduce_sum | solution.py:44
  163.3 4.6 %all-to-all-done = f32[4,16,2,2,256]{4,1,3,2,0:T(8,128)S(1)} async-done(((f32[4,16,2,2,256]{4,1,3,2,0:T(8,128)}), f32[4,16,2,2,256]{4,1,3,2,0:T(8,128)S(1)}, u32[]{:S(2)}, u32[]{:S(2)}) %all-to-all-start) | async-done | bytes 262176 | tf_op jit(solution)/shard_map/all_to_all | solution.py:43
  167.9 0.7 copy.76
  (13 shorter events, 0.1 us)
Async XLA Ops:
  7.2 60.6 %copy-start = (bf16[256,2,2,256]{3,2,1,0:T(2,128)(2,1)S(1)}, bf16[256,2,2,256]{3,2,1,0:T(2,128)(2,1)}, u32[]{:S(2)}) copy-start(bf16[256,2,2,256]{3,2,1,0:T(2,128)(2,1)} %param.9) | copy-start | bytes 1572868
  9.9 9.2 %copy-start.3 = (s32[256,2,32]{0,2,1:T(8,128)S(1)}, s32[256,2,32]{0,2,1:T(8,128)}, u32[]{:S(2)}) copy-start(s32[256,2,32]{0,2,1:T(8,128)} %param.13) | copy-start | bytes 196612
  9.9 9.2 %copy-start.4 = (f32[256,2,32]{0,2,1:T(8,128)S(1)}, f32[256,2,32]{0,2,1:T(8,128)}, u32[]{:S(2)}) copy-start(f32[256,2,32]{0,2,1:T(8,128)} %param.14) | copy-start | bytes 196612
  9.9 9.2 %copy-start.5 = (f32[256,2,32]{0,2,1:T(8,128)S(1)}, f32[256,2,32]{0,2,1:T(8,128)}, u32[]{:S(2)}) copy-start(f32[256,2,32]{0,2,1:T(8,128)} %param.15) | copy-start | bytes 196612
  9.9 10.4 %copy-start.2 = (s32[256,2,2,32]{0,3,2,1:T(8,128)S(1)}, s32[256,2,2,32]{0,3,2,1:T(8,128)}, u32[]{:S(2)}) copy-start(s32[256,2,2,32]{0,3,2,1:T(8,128)} %param.12) | copy-start | bytes 393220
  9.9 62.9 %all-to-all-start.1 = ((bf16[4,256,2,2,256]{4,1,3,2,0:T(8,128)(2,1)}), bf16[4,256,2,2,256]{4,1,3,2,0:T(8,128)(2,1)S(1)}, u32[]{:S(2)}, u32[]{:S(2)}) async-start(bf16[4,256,2,2,256]{4,1,3,2,0:T(8,128)(2,1)} %broadcast_in_dim.24), calls=%async_computation.3 | async-start | bytes 4194304 | tf_op jit(solution)/shard_map/all_to_all | solution.py:16
  19.1 105.2 %reduce-scatter.3.cloned.1.call-start = ((), (), s32[]{:S(2)}) async-start(), calls=%async_computation.5 | async-start | bytes 5242880 | tf_op jit(solution)/shard_map/reduce_scatter | solution.py:32
  72.8 1.6 copy-start.1
  83.9 69.2 %all-to-all-start.2 = ((f32[4,64,4096]{2,1,0:T(8,128)}), f32[4,64,4096]{2,1,0:T(8,128)}, u32[]{:S(2)}, u32[]{:S(2)}) async-start(f32[4,64,4096]{2,1,0:T(8,128)} %fusion.2), calls=%async_computation.4 | async-start | bytes 8388608 | tf_op jit(solution)/shard_map/all_to_all | solution.py:43
  90.0 61.5 %reduce-scatter.5.cloned.1.call-start = ((), (), s32[]{:S(2)}) async-start(), calls=%async_computation.6 | async-start | bytes 1310720 | tf_op jit(solution)/shard_map/reduce_scatter | solution.py:32
  153.1 14.7 %all-to-all-start = ((f32[4,16,2,2,256]{4,1,3,2,0:T(8,128)}), f32[4,16,2,2,256]{4,1,3,2,0:T(8,128)S(1)}, u32[]{:S(2)}, u32[]{:S(2)}) async-start(f32[4,16,2,2,256]{4,1,3,2,0:T(8,128)} %copy.70), calls=%async_computation.2 | async-start | bytes 524288 | tf_op jit(solution)/shard_map/all_to_all | solution.py:43
Sparse Core Ops, SparseCore 0:
  72.9 51.3 reduce-scatter.2
  126.9 24.5 reduce-scatter.4
where the time goes:
time: 179 us; the launch traced here: 175 us
  waiting for transfers between devices  66.1 us (37%)
  other arithmetic  33.8 us (19%)
  local copies, waits for them, and re-layouts  25.7 us (14%)
  starting transfers between devices  22 us (12%)
  between operations  14.1 us (8%)
  matrix products  13.6 us (8%)
    reduce_scatter x2, waiting for transfers between devices, summed_rows(): total = lax.psum_scatter(total, axis, scatter_dimension=0, tiled=True)  61.5 us
    reduce_sum x8, other arithmetic, build_rows(): jnp.sum(jnp.where(match, val_here[:, :, None], 0.0), axis=1)  29.6 us
    all_to_all x2, starting transfers between devices, sum_at_owner(): tiles = lax.all_to_all(in_blocks(x, dim, devices), axis, 0, 0, tiled=True)  12.9 us
    all_to_all x1, starting transfers between devices, copy_for_each(): return lax.all_to_all(copies, axis, split_axis=0, concat_axis=0, tiled=True)  9.14 us
    dot_general x1, matrix products, on_device(): lax.dot_general(part_rows, query_weight, (((1,), (1,)), ((), ())), prefer...  7.72 us
    eq x8, local copies, waits for them, and re-layouts, build_rows(): match = idx_here[:, :, None] == row_ids[None, None, :]  6.75 us
    dynamic_update_slice x8, local copies, waits for them, and re-layouts, on_device(): lax.map(build_rows, (idx_blocks, val_blocks))  5.85 us
    dot_general x1, matrix products, on_device(): jnp.einsum('thxr,thxf->rhxf', part_rows, queries, preferred_element_type=...  5.05 us
  transfers between devices with their start and end apart: 5, of which 3 were waited for; matrix products, arithmetic and copies ran while one was open for 39% of the time, Pallas kernels for 0%

commit v1 on v0

v1 whole, which is shorter than its diff:
```python
import functools

import jax
import jax.numpy as jnp
from jax import lax
from jax.experimental import pallas as pl
from jax.experimental.pallas import tpu as pltpu
from jax.sharding import Mesh
from jax.sharding import PartitionSpec as P

DP_KEY = ("dp_0", "dp_1", "key")
DP_KEY_TENSOR = ("dp_0", "dp_1", "key", "tensor")
AXES = ("dp_0", "dp_1", "key", "tensor")
MESH = pl.DeviceIdType.MESH
F32 = jnp.float32
BF16 = jnp.bfloat16
CHUNKS = 8
MESSAGES = 96


def kernel(
    idx_ref, pair_ref, w_ref, wg_ref, q_ref, ks_ref, wq_ref,
    key_out, in_out,
    idxf, val, score, first, second, table, part, kbuf, wv, qg,
    r1, s3, res1, r2, s23, res2, r3, po, c1, c2s, c2r,
    w_sem, send_sem, recv_sem,
):
    y, x, k, t = (lax.axis_index(a) for a in AXES)
    zl, c = t // 2, lax.rem(t, 2)
    coord = {"dp_0": y, "dp_1": x, "key": k}

    def at(axis, step):
        return lax.rem(coord[axis] + step + 4, 4)

    def near(axis, step):
        return {axis: at(axis, step)}

    other_core = {"tensor": zl * 2 + (1 - c)}
    other_chip = {"tensor": (1 - zl) * 2 + c}

    barrier = pltpu.get_barrier_semaphore()
    partners = [near(a, s) for a in ("dp_0", "dp_1") for s in (1, -1)]
    partners += [near("key", s) for s in (1, -1, 2)] + [other_core, other_chip]
    for device in partners:
        pl.semaphore_signal(barrier, inc=1, device_id=device, device_id_type=MESH)
    pl.semaphore_wait(barrier, len(partners))

    names, sent = {}, []

    def number(name):
        return names.setdefault(name, len(names))

    def copy(name, src, dst, device):
        n = number(name)
        return pltpu.make_async_remote_copy(
            src_ref=src, dst_ref=dst, send_sem=send_sem.at[n], recv_sem=recv_sem.at[n],
            device_id=device, device_id_type=MESH,
        )

    def send(name, src, dst, device):
        one = copy(name, src, dst, device)
        one.start()
        sent.append(one)

    def arrived(name, dst):
        copy(name, dst, dst, other_core).wait_recv()

    wide = wv.shape[0] // CHUNKS
    loads = [
        pltpu.make_async_copy(wq_ref.at[pl.ds(j * wide, wide)], wv.at[pl.ds(j * wide, wide)], w_sem.at[j])
        for j in range(CHUNKS)
    ]
    for load in loads:
        load.start()

    rows = kbuf.shape[2] // 4
    spread = (("dp_1", 0), ("dp_0", 2))

    def quarter(axis, step=0):
        return pl.ds(pl.multiple_of(at(axis, step) * rows, rows), rows)

    for axis, h0 in spread:
        mine = quarter(axis)
        for slot, step in ((0, 1), (1, -1)):
            send(("z1", h0, slot), ks_ref.at[pl.ds(h0, 2), mine], kbuf.at[slot, pl.ds(h0, 2), mine], near("key", step))

    def key_second():
        for axis, h0 in spread:
            mine = quarter(axis)
            for slot in (0, 1):
                arrived(("z1", h0, slot), kbuf.at[slot, pl.ds(h0, 2), mine])
            for slot, step in ((0, 1), (1, -1)):
                send(("z2", h0, slot), kbuf.at[slot, h0 + slot, mine], kbuf.at[2, h0 + slot, mine], near("key", step))

    def share_first(slot):
        for axis, h0 in spread:
            mine = quarter(axis)
            block = kbuf.at[slot, pl.ds(h0, 2), mine]
            if slot == 2:
                for side in (0, 1):
                    arrived(("z2", h0, side), kbuf.at[2, h0 + side, mine])
            for side, step in ((0, 1), (1, -1)):
                send(("g1", h0, slot, side), block, block, near(axis, step))

    def share_second(slot):
        for axis, h0 in spread:
            for side, step in ((0, 1), (1, -1)):
                theirs = quarter(axis, -step)
                arrived(("g1", h0, slot, side), kbuf.at[slot, pl.ds(h0, 2), theirs])
                half = kbuf.at[slot, h0 + side, theirs]
                send(("g2", h0, slot, side), half, half, near(axis, step))

    def share_end(slot):
        for axis, h0 in spread:
            for side in (0, 1):
                arrived(("g2", h0, slot, side), kbuf.at[slot, h0 + side, quarter(axis, 2)])

    kept, tokens = idx_ref.shape[1], idx_ref.shape[2]
    for hx in range(4):
        idxf[hx] = idx_ref[hx].astype(F32)
    slots = lax.broadcasted_iota(jnp.int32, (kept, tokens), 0)
    for h in range(2):
        product = w_ref[h] * wg_ref[h]
        total = jnp.sum(product, axis=0, keepdims=True)
        score[...] = w_ref[h] * (wg_ref[h] - total)
        first[...] = pair_ref[h] >> 5
        second[...] = pair_ref[h] & 31

        def add_pairs(step, sums):
            one, two = sums
            for sub in range(4):
                row = pl.ds(step * 4 + sub, 1)
                here = score[row, :]
                one = one + jnp.where(slots == first[row, :], here, 0.0)
                two = two + jnp.where(slots == second[row, :], here, 0.0)
            return one, two

        zero = jnp.zeros((kept, tokens), F32)
        one, two = lax.fori_loop(0, kept // 4, add_pairs, (zero, zero))
        val[2 * h] = one
        val[2 * h + 1] = two

    across = 128
    ids = lax.broadcasted_iota(jnp.int32, (16, 16, across), 0) * 16 + lax.broadcasted_iota(jnp.int32, (16, 16, across), 1)
    ids = ids.astype(F32).astype(BF16)

    def build(hx):
        @pl.loop(0, 4)
        def _(b):
            low = (b * 256).astype(F32)
            for lane in range(tokens // across):
                cols = slice(lane * across, (lane + 1) * across)
                acc = jnp.zeros((16, 16, across), BF16)
                for a in range(kept):
                    place = jnp.broadcast_to(idxf[hx, a : a + 1, cols] - low, (16, across)).astype(BF16)
                    value = jnp.broadcast_to(val[hx, a : a + 1, cols], (16, across)).astype(BF16)
                    acc = jnp.where(ids == place[None], value[None], acc)
                table[hx, b, :, cols] = acc.reshape(256, across)
            grad = jnp.dot(table[hx, b], q_ref[hx], preferred_element_type=F32)
            part[hx, b] = grad.astype(BF16).reshape(4, 64, grad.shape[1])

    def way(hx):
        return 1 - 2 * (hx % 2)

    def block(stage, hx, step):
        if stage == 2:
            return res1.at[hx, at("dp_0" if hx < 2 else "dp_1", step)]
        if hx < 2:
            return part.at[hx, :, at("dp_1", step)]
        return part.at[hx, at("dp_0", step)]

    def axis_of(stage, hx):
        return "dp_1" if (hx < 2) == (stage == 1) else "dp_0"

    into = {1: r1, 2: r2}
    staged = {1: s3, 2: s23}

    def reduce_first(stage, hx):
        axis, d = axis_of(stage, hx), way(hx)
        send((stage, hx, 0), block(stage, hx, 2), into[stage].at[hx, 0], near(axis, d))
        send((stage, hx, 1), block(stage, hx, -d), into[stage].at[hx, 1], near(axis, -d))

    def reduce_second(stage, hx):
        axis, d = axis_of(stage, hx), way(hx)
        arrived((stage, hx, 0), into[stage].at[hx, 0])
        both = block(stage, hx, d)[...].astype(F32) + into[stage][hx, 0].astype(F32)
        staged[stage][hx] = both.astype(BF16)
        send((stage, hx, 2), staged[stage].at[hx], into[stage].at[hx, 2], near(axis, d))

    def reduce_end(stage, hx):
        got = into[stage]
        arrived((stage, hx, 1), got.at[hx, 1])
        arrived((stage, hx, 2), got.at[hx, 2])
        total = block(stage, hx, 0)[...].astype(F32) + got[hx, 1].astype(F32) + got[hx, 2].astype(F32)
        if stage == 1:
            res1[hx] = total.astype(BF16)
        else:
            res2[:, hx] = total.astype(BF16).reshape(4, 16, total.shape[-1])

    key_steps = (1, -1, 2)

    build(0)
    reduce_first(1, 0)
    build(1)
    reduce_first(1, 1)
    build(2)
    reduce_first(1, 2)
    key_second()
    share_first(0)
    share_first(1)
    build(3)
    reduce_first(1, 3)
    share_first(2)
    share_second(0)
    share_second(1)
    for hx in range(4):
        reduce_second(1, hx)
    share_second(2)
    for slot in range(3):
        share_end(slot)

    transposed = (((0,), (0,)), ((), ()))
    for hx in range(4):
        total = lax.dot_general(table[hx, k], ks_ref[hx], transposed, preferred_element_type=F32)
        for slot, step in ((0, -1), (1, 1), (2, 2)):
            total += lax.dot_general(table[hx, at("key", step)], kbuf[slot, hx], transposed, preferred_element_type=F32)
        qg[:, hx * 256 : (hx + 1) * 256] = total.astype(BF16)

    def project(j):
        loads[j].wait()
        out = lax.dot_general(qg[...], wv[j * wide : (j + 1) * wide], (((1,), (1,)), ((), ())), preferred_element_type=F32)
        po[j] = out.astype(BF16).reshape(2, 2, 64, wide)
        send(("c1", j), po.at[j, :, 1 - c], c1.at[j], other_core)

    def pass_on(j):
        arrived(("c1", j), c1.at[j])
        c2s[j] = (po[j, 1 - zl, c].astype(F32) + c1[j, 1 - zl].astype(F32)).astype(BF16)
        send(("c2", j), c2s.at[j], c2r.at[j], other_chip)

    for j in range(CHUNKS):
        project(j)
        if j >= 2:
            pass_on(j - 2)
    pass_on(CHUNKS - 2)
    pass_on(CHUNKS - 1)
    for hx in range(4):
        reduce_end(1, hx)
        reduce_first(2, hx)
    for hx in range(4):
        reduce_second(2, hx)
    for hx in range(4):
        reduce_end(2, hx)
    for n, step in enumerate(key_steps):
        send((3, n), res2.at[at("key", step)], r3.at[n], near("key", step))
    for j in range(CHUNKS):
        arrived(("c2", j), c2r.at[j])
        total = po[j, zl, c].astype(F32) + c1[j, zl].astype(F32) + c2r[j].astype(F32)
        in_out[:, j * wide : (j + 1) * wide] = total.astype(BF16)
    total = res2[k].astype(F32)
    for n in range(3):
        arrived((3, n), r3.at[n])
        total = total + r3[n].astype(F32)
    key_out[...] = total
    for one in sent:
        one.wait_send()


def on_device(queries, sub_keys, query_weight, sub_choice, pair_choice, weights, weight_grad):
    tok, heads, halves, width = queries.shape
    topk = pair_choice.shape[2]
    groups = heads * halves
    rows = sub_keys.shape[0]
    model = query_weight.shape[0]
    wide = model // CHUNKS
    idx = jnp.transpose(sub_choice, (1, 2, 3, 0)).reshape(groups, topk, tok)
    pair, w, wg = (jnp.transpose(v, (1, 2, 0)) for v in (pair_choice, weights, weight_grad))
    q = jnp.transpose(queries.reshape(tok, groups, width), (1, 0, 2))
    ks = jnp.transpose(sub_keys.reshape(rows, groups, width), (1, 0, 2))
    vmem = pl.BlockSpec(memory_space=pltpu.VMEM)
    key_grad, in_grad = pl.pallas_call(
        kernel,
        out_shape=(
            jax.ShapeDtypeStruct((groups, 16, width), F32),
            jax.ShapeDtypeStruct((tok // 4, model), BF16),
        ),
        in_specs=[vmem] * 6 + [pl.BlockSpec(memory_space=pl.ANY)],
        out_specs=(vmem, vmem),
        scratch_shapes=[
            pltpu.VMEM((groups, topk, tok), F32),
            pltpu.VMEM((groups, topk, tok), F32),
            pltpu.VMEM((topk, tok), F32),
            pltpu.VMEM((topk, tok), jnp.int32),
            pltpu.VMEM((topk, tok), jnp.int32),
            pltpu.VMEM((groups, 4, rows, tok), BF16),
            pltpu.VMEM((groups, 4, 4, 64, width), BF16),
            pltpu.VMEM((3, groups, rows, width), BF16),
            pltpu.VMEM((model, groups * width), BF16),
            pltpu.VMEM((tok, groups * width), BF16),
            pltpu.VMEM((groups, 3, 4, 64, width), BF16),
            pltpu.VMEM((groups, 4, 64, width), BF16),
            pltpu.VMEM((groups, 4, 64, width), BF16),
            pltpu.VMEM((groups, 3, 64, width), BF16),
            pltpu.VMEM((groups, 64, width), BF16),
            pltpu.VMEM((4, groups, 16, width), BF16),
            pltpu.VMEM((3, groups, 16, width), BF16),
            pltpu.VMEM((CHUNKS, 2, 2, 64, wide), BF16),
            pltpu.VMEM((CHUNKS, 2, 64, wide), BF16),
            pltpu.VMEM((CHUNKS, 64, wide), BF16),
            pltpu.VMEM((CHUNKS, 64, wide), BF16),
            pltpu.SemaphoreType.DMA((CHUNKS,)),
            pltpu.SemaphoreType.DMA((MESSAGES,)),
            pltpu.SemaphoreType.DMA((MESSAGES,)),
        ],
        compiler_params=pltpu.CompilerParams(
            collective_id=0, has_side_effects=True, vmem_limit_bytes=48 * 2**20
        ),
    )(idx, pair, w, wg, q, ks, query_weight)
    sub_key_grad = jnp.transpose(key_grad, (1, 0, 2)).reshape(16, heads, halves, width)
    return sub_key_grad, in_grad


def solution(mesh):
    split = Mesh(
        mesh.devices.reshape(4, 4, mesh.shape["key"], mesh.shape["tensor"]), AXES
    )
    in_specs = (
        P(DP_KEY, "tensor", None, None),
        P("key", "tensor", None, None),
        P(None, "tensor"),
        P(DP_KEY, "tensor", None, None),
        P(DP_KEY, "tensor", None),
        P(DP_KEY, "tensor", None),
        P(DP_KEY, "tensor", None),
    )
    out_specs = (P(DP_KEY, "tensor", None, None), P(DP_KEY_TENSOR, None))
    return jax.shard_map(
        on_device, mesh=split, in_specs=in_specs, out_specs=out_specs, check_vma=False
    )
```

time: 179 us -> 61.8 us (0.35); the launches traced: 175 us -> 61.5 us
  waiting for transfers between devices: 66.1 us -> 0 us
  Pallas kernels: 0 us -> 53.7 us
  other arithmetic: 33.8 us -> 0 us
  starting transfers between devices: 22 us -> 0 us
  local copies, waits for them, and re-layouts: 25.7 us -> 7.12 us
  matrix products: 13.6 us -> 0 us
  between operations: 14.1 us -> 0.66 us
    reduce_scatter x2 -> x0, waiting for transfers between devices: 61.5 us -> none  [summed_rows(): total = lax.psum_scatter(total, axis, scatter_dimension=0, tiled=True)]
    pallas_call x0 -> x1, Pallas kernels: none -> 53.7 us  [on_device(): pl.pallas_call(kernel, out_shape=(jax.ShapeDtypeStruct((groups, 16, width...]
    reduce_sum x11 -> x0, other arithmetic: 33.6 us -> none  [the longest x8 29.6 us: build_rows(): jnp.sum(jnp.where(match, val_here[:, :, None], 0.0), axis=1)]
    all_to_all x3 -> x0, starting transfers between devices: 22 us -> none  [the longest x2 12.9 us: sum_at_owner(): tiles = lax.all_to_all(in_blocks(x, dim, devices), axis, 0, 0, tiled=True)]
    dot_general x3 -> x0, matrix products: 13.6 us -> none  [the longest x1 7.72 us: on_device(): lax.dot_general(part_rows, query_weight, (((1,), (1,)), ((), ())), prefer...]
    eq x8 -> x0, local copies, waits for them, and re-layouts: 6.75 us -> none  [build_rows(): match = idx_here[:, :, None] == row_ids[None, None, :]]
    dynamic_update_slice x8 -> x0, local copies, waits for them, and re-layouts: 5.85 us -> none  [on_device(): lax.map(build_rows, (idx_blocks, val_blocks))]
    reshape x2 -> x0, local copies, waits for them, and re-layouts: 5.8 us -> none  [the longest x1 4.13 us: on_device(): lax.map(build_rows, (idx_blocks, val_blocks))]
  transfers between devices with their start and end apart: 5 -> 0, of which waited for: 3 -> 0; matrix products, arithmetic and copies ran while one was open for 39% -> 0% of each run, Pallas kernels for 0% -> 0%
where the time goes in v1:
time: 61.8 us; the launch traced here: 61.5 us
  Pallas kernels  53.7 us (87%)
  local copies, waits for them, and re-layouts  7.12 us (12%)
  between operations  0.66 us (1%)
    pallas_call x1, Pallas kernels, on_device(): pl.pallas_call(kernel, out_shape=(jax.ShapeDtypeStruct((groups, 16, width...  53.7 us
    unnamed x12, local copies, waits for them, and re-layouts  7.12 us

profile of v1, /device:TPU:1, one launch (start us, length us, event | category | flops | bytes accessed | tf_op | source)
XLA Modules:
  0.0 61.5 jit_solution(17440468919725657939)
XLA Ops:
  0.6 1.1 %copy.9 = bf16[256,2,2,256]{3,0,2,1:T(8,128)(2,1)S(1)} copy(bf16[256,2,2,256]{3,2,1,0:T(2,128)(2,1)} %param.7) | data formatting | bytes 1048576 | tf_op args[0]
  1.7 1.1 %copy.10 = bf16[256,2,2,256]{3,0,2,1:T(8,128)(2,1)S(1)} copy(bf16[256,2,2,256]{3,2,1,0:T(2,128)(2,1)} %param.8) | data formatting | bytes 1048576 | tf_op args[1]
  2.9 0.0 copy-start
  2.9 0.9 %copy-done = s32[256,2,2,32]{0,3,2,1:T(8,128)S(1)} copy-done((s32[256,2,2,32]{0,3,2,1:T(8,128)S(1)}, s32[256,2,2,32]{0,3,2,1:T(8,128)}, u32[]{:S(2)}) %copy-start) | copy-done | bytes 131096
  3.8 0.0 copy-start.1
  3.8 0.8 %copy-done.1 = s32[256,2,32]{0,2,1:T(8,128)S(1)} copy-done((s32[256,2,32]{0,2,1:T(8,128)S(1)}, s32[256,2,32]{0,2,1:T(8,128)}, u32[]{:S(2)}) %copy-start.1) | copy-done | bytes 65560
  4.6 0.0 copy-start.2
  4.6 0.8 %copy-done.2 = f32[256,2,32]{0,2,1:T(8,128)S(1)} copy-done((f32[256,2,32]{0,2,1:T(8,128)S(1)}, f32[256,2,32]{0,2,1:T(8,128)}, u32[]{:S(2)}) %copy-start.2) | copy-done | bytes 65560
  5.5 0.0 copy-start.3
  5.5 0.8 %copy-done.3 = f32[256,2,32]{0,2,1:T(8,128)S(1)} copy-done((f32[256,2,32]{0,2,1:T(8,128)S(1)}, f32[256,2,32]{0,2,1:T(8,128)}, u32[]{:S(2)}) %copy-start.3) | copy-done | bytes 65560
  6.3 53.7 %shard_map.86 = (f32[4,16,256]{2,1,0:T(8,128)S(1)}, bf16[64,4096]{1,0:T(8,128)(2,1)S(1)}) custom-call(s32[4,32,256]{2,1,0:T(8,128)S(1)} %bitcast.17, s32[2,32,256]{2,1,0:T(8,128)S(1)} %bitcast.18, f32[2,32,256]{2,1,0:T(8,128)S(1)} %bitcast.19, f32[2,32,256]{2,1,0:T(8,128)S(1)} %bitcast.20, bf16[4,256,256]{2,1,0:T(8,128)(2,1)S(1)} %bitcast.15, ...), custom_call_target="tpu_custom_call" | custom-call | tf_op jit(solution)/shard_map/pallas_call | solution.py:280
  60.0 0.7 %copy.11 = f32[16,2,2,256]{3,2,1,0:T(2,128)} copy(f32[16,2,2,256]{3,0,2,1:T(8,128)S(1)} %bitcast.21) | data formatting | bytes 131072
  60.7 0.8 %copy.13 = bf16[64,4096]{1,0:T(8,128)(2,1)} copy(bf16[64,4096]{1,0:T(8,128)(2,1)S(1)} %get-tuple-element.11) | data formatting | bytes 1048576
Async XLA Ops:
  2.9 0.9 %copy-start = (s32[256,2,2,32]{0,3,2,1:T(8,128)S(1)}, s32[256,2,2,32]{0,3,2,1:T(8,128)}, u32[]{:S(2)}) copy-start(s32[256,2,2,32]{0,3,2,1:T(8,128)} %param.10) | copy-start | bytes 393220
  3.8 0.8 %copy-start.1 = (s32[256,2,32]{0,2,1:T(8,128)S(1)}, s32[256,2,32]{0,2,1:T(8,128)}, u32[]{:S(2)}) copy-start(s32[256,2,32]{0,2,1:T(8,128)} %param.11) | copy-start | bytes 196612
  4.6 0.8 %copy-start.2 = (f32[256,2,32]{0,2,1:T(8,128)S(1)}, f32[256,2,32]{0,2,1:T(8,128)}, u32[]{:S(2)}) copy-start(f32[256,2,32]{0,2,1:T(8,128)} %param.12) | copy-start | bytes 196612
  5.5 0.8 %copy-start.3 = (f32[256,2,32]{0,2,1:T(8,128)S(1)}, f32[256,2,32]{0,2,1:T(8,128)}, u32[]{:S(2)}) copy-start(f32[256,2,32]{0,2,1:T(8,128)} %param.13) | copy-start | bytes 196612

commit v2 on v1

--- a/solution.py
+++ b/solution.py
@@ -19,11 +19,12 @@
 
 
 def kernel(
-    idx_ref, pair_ref, w_ref, wg_ref, q_ref, ks_ref, wq_ref,
+    idx_hbm, pair_hbm, w_hbm, wg_hbm, q_hbm, ks_hbm, wq_ref,
     key_out, in_out,
-    idxf, val, score, first, second, table, part, kbuf, wv, qg,
+    idx_ref, pair_ref, w_ref, wg_ref, q_raw, ks_raw, q_ref, ks_ref,
+    idxf, val, score, first, second, table, part, kbuf, wv, qg, qsum,
     r1, s3, res1, r2, s23, res2, r3, po, c1, c2s, c2r,
-    w_sem, send_sem, recv_sem,
+    w_sem, in_sem, send_sem, recv_sem,
 ):
     y, x, k, t = (lax.axis_index(a) for a in AXES)
     zl, c = t // 2, lax.rem(t, 2)
@@ -43,28 +44,16 @@
     partners += [near("key", s) for s in (1, -1, 2)] + [other_core, other_chip]
     for device in partners:
         pl.semaphore_signal(barrier, inc=1, device_id=device, device_id_type=MESH)
-    pl.semaphore_wait(barrier, len(partners))
-
-    names, sent = {}, []
-
-    def number(name):
-        return names.setdefault(name, len(names))
-
-    def copy(name, src, dst, device):
-        n = number(name)
-        return pltpu.make_async_remote_copy(
-            src_ref=src, dst_ref=dst, send_sem=send_sem.at[n], recv_sem=recv_sem.at[n],
-            device_id=device, device_id_type=MESH,
-        )
-
-    def send(name, src, dst, device):
-        one = copy(name, src, dst, device)
+
+    fetched = [
+        pltpu.make_async_copy(src, dst, in_sem.at[n])
+        for n, (src, dst) in enumerate((
+            (ks_hbm, ks_raw), (w_hbm, w_ref), (wg_hbm, wg_ref),
+            (pair_hbm, pair_ref), (idx_hbm, idx_ref), (q_hbm, q_raw),
+        ))
+    ]
+    for one in fetched:
         one.start()
-        sent.append(one)
-
-    def arrived(name, dst):
-        copy(name, dst, dst, other_core).wait_recv()
-
     wide = wv.shape[0] // CHUNKS
     loads = [
         pltpu.make_async_copy(wq_ref.at[pl.ds(j * wide, wide)], wv.at[pl.ds(j * wide, wide)], w_sem.at[j])
@@ -72,48 +61,82 @@
     ]
     for load in loads:
         load.start()
+    fetched[0].wait()
+    for hx in range(4):
+        ks_ref[hx] = ks_raw[:, hx // 2, hx % 2, :]
+    pl.semaphore_wait(barrier, len(partners))
+
+    names, sent = {}, []
+
+    def copy(name, src, dst, device):
+        n = names.setdefault(name, len(names))
+        return pltpu.make_async_remote_copy(
+            src_ref=src, dst_ref=dst, send_sem=send_sem.at[n], recv_sem=recv_sem.at[n],
+            device_id=device, device_id_type=MESH,
+        )
+
+    def send(name, src, dst, device):
+        one = copy(name, src, dst, device)
+        one.start()
+        sent.append(one)
+
+    def arrived(name, dst):
+        copy(name, dst, dst, other_core).wait_recv()
+
+    def way(hx):
+        return 1 - 2 * (hx % 2)
 
     rows = kbuf.shape[2] // 4
-    spread = (("dp_1", 0), ("dp_0", 2))
-
-    def quarter(axis, step=0):
-        return pl.ds(pl.multiple_of(at(axis, step) * rows, rows), rows)
-
-    for axis, h0 in spread:
-        mine = quarter(axis)
-        for slot, step in ((0, 1), (1, -1)):
-            send(("z1", h0, slot), ks_ref.at[pl.ds(h0, 2), mine], kbuf.at[slot, pl.ds(h0, 2), mine], near("key", step))
+
+    def ring(hx):
+        return "dp_1" if hx < 2 else "dp_0"
+
+    def quarter(hx, step=0):
+        return pl.ds(pl.multiple_of(at(ring(hx), step) * rows, rows), rows)
+
+    def key_first(late):
+        for hx in range(4):
+            d = -way(hx) if late else way(hx)
+            slot = (1 - d) // 2
+            send(("z1", slot, hx), ks_ref.at[hx, quarter(hx)], kbuf.at[slot, hx, quarter(hx)], near("key", d))
 
     def key_second():
-        for axis, h0 in spread:
-            mine = quarter(axis)
-            for slot in (0, 1):
-                arrived(("z1", h0, slot), kbuf.at[slot, pl.ds(h0, 2), mine])
-            for slot, step in ((0, 1), (1, -1)):
-                send(("z2", h0, slot), kbuf.at[slot, h0 + slot, mine], kbuf.at[2, h0 + slot, mine], near("key", step))
-
-    def share_first(slot):
-        for axis, h0 in spread:
-            mine = quarter(axis)
-            block = kbuf.at[slot, pl.ds(h0, 2), mine]
-            if slot == 2:
-                for side in (0, 1):
-                    arrived(("z2", h0, side), kbuf.at[2, h0 + side, mine])
-            for side, step in ((0, 1), (1, -1)):
-                send(("g1", h0, slot, side), block, block, near(axis, step))
-
-    def share_second(slot):
-        for axis, h0 in spread:
-            for side, step in ((0, 1), (1, -1)):
-                theirs = quarter(axis, -step)
-                arrived(("g1", h0, slot, side), kbuf.at[slot, pl.ds(h0, 2), theirs])
-                half = kbuf.at[slot, h0 + side, theirs]
-                send(("g2", h0, slot, side), half, half, near(axis, step))
+        for hx in range(4):
+            d = way(hx)
+            slot = (1 - d) // 2
+            piece = kbuf.at[slot, hx, quarter(hx)]
+            arrived(("z1", slot, hx), piece)
+            send(("z2", hx), piece, kbuf.at[2, hx, quarter(hx)], near("key", d))
+
+    def share_first(slot, hx, name=None):
+        piece = kbuf.at[slot, hx, quarter(hx)]
+        if name is not None:
+            arrived(name, piece)
+        for d in (way(hx), -way(hx)):
+            send(("g1", slot, hx, d), piece, piece, near(ring(hx), d))
+
+    def share_second(slot, hx):
+        d = way(hx)
+        piece = kbuf.at[slot, hx, quarter(hx, -d)]
+        arrived(("g1", slot, hx, d), piece)
+        send(("g2", slot, hx), piece, piece, near(ring(hx), d))
 
     def share_end(slot):
-        for axis, h0 in spread:
-            for side in (0, 1):
-                arrived(("g2", h0, slot, side), kbuf.at[slot, h0 + side, quarter(axis, 2)])
+        for hx in range(4):
+            d = way(hx)
+            arrived(("g1", slot, hx, -d), kbuf.at[slot, hx, quarter(hx, d)])
+            arrived(("g2", slot, hx), kbuf.at[slot, hx, quarter(hx, 2)])
+
+    def early(hx):
+        return (1 - way(hx)) // 2
+
+    key_first(False)
+    key_first(True)
+
+    for one in fetched[1:]:
+        one.wait()
+    for hx in range(4):
+        q_ref[hx] = q_raw[:, hx // 2, hx % 2, :]
 
     kept, tokens = idx_ref.shape[1], idx_ref.shape[2]
     for hx in range(4):
@@ -159,9 +182,6 @@
             grad = jnp.dot(table[hx, b], q_ref[hx], preferred_element_type=F32)
             part[hx, b] = grad.astype(BF16).reshape(4, 64, grad.shape[1])
 
-    def way(hx):
-        return 1 - 2 * (hx % 2)
-
     def block(stage, hx, step):
         if stage == 2:
             return res1.at[hx, at("dp_0" if hx < 2 else "dp_1", step)]
@@ -201,29 +221,41 @@
 
     build(0)
     reduce_first(1, 0)
+    key_second()
+    for hx in range(4):
+        share_first(early(hx), hx)
+    build(2)
+    reduce_first(1, 2)
+    for hx in range(4):
+        share_first(1 - early(hx), hx, ("z1", 1 - early(hx), hx))
     build(1)
     reduce_first(1, 1)
-    build(2)
-    reduce_first(1, 2)
-    key_second()
-    share_first(0)
-    share_first(1)
+    for hx in range(4):
+        share_second(early(hx), hx)
+    for hx in (0, 2):
+        reduce_second(1, hx)
+    for hx in range(4):
+        share_first(2, hx, ("z2", hx))
+    for hx in range(4):
+        share_second(1 - early(hx), hx)
     build(3)
     reduce_first(1, 3)
-    share_first(2)
-    share_second(0)
-    share_second(1)
-    for hx in range(4):
-        reduce_second(1, hx)
-    share_second(2)
-    for slot in range(3):
-        share_end(slot)
+    for hx in range(4):
+        share_second(2, hx)
+    share_end(0)
+    share_end(1)
 
     transposed = (((0,), (0,)), ((), ()))
-    for hx in range(4):
-        total = lax.dot_general(table[hx, k], ks_ref[hx], transposed, preferred_element_type=F32)
-        for slot, step in ((0, -1), (1, 1), (2, 2)):
-            total += lax.dot_general(table[hx, at("key", step)], kbuf[slot, hx], transposed, preferred_element_type=F32)
+
+    def shard_term(hx, step, shard):
+        return lax.dot_general(table[hx, at("key", step)], shard, transposed, preferred_element_type=F32)
+
+    for hx in range(4):
+        qsum[hx] = shard_term(hx, 0, ks_ref[hx]) + shard_term(hx, -1, kbuf[0, hx]) + shard_term(hx, 1, kbuf[1, hx])
+    reduce_second(1, 1)
+    share_end(2)
+    for hx in range(4):
+        total = qsum[hx] + shard_term(hx, 2, kbuf[2, hx])
         qg[:, hx * 256 : (hx + 1) * 256] = total.astype(BF16)
 
     def project(j):
@@ -241,14 +273,17 @@
         project(j)
         if j >= 2:
             pass_on(j - 2)
+        if j == 2:
+            reduce_second(1, 3)
+        if j >= CHUNKS - 4:
+            hx = (0, 2, 1, 3)[j - CHUNKS + 4]
+            reduce_end(1, hx)
+            reduce_first(2, hx)
     pass_on(CHUNKS - 2)
     pass_on(CHUNKS - 1)
-    for hx in range(4):
-        reduce_end(1, hx)
-        reduce_first(2, hx)
-    for hx in range(4):
+    for hx in (0, 2, 1, 3):
         reduce_second(2, hx)
-    for hx in range(4):
+    for hx in (0, 2, 1, 3):
         reduce_end(2, hx)
     for n, step in enumerate(key_steps):
         send((3, n), res2.at[at("key", step)], r3.at[n], near("key", step))
@@ -274,8 +309,6 @@
     wide = model // CHUNKS
     idx = jnp.transpose(sub_choice, (1, 2, 3, 0)).reshape(groups, topk, tok)
     pair, w, wg = (jnp.transpose(v, (1, 2, 0)) for v in (pair_choice, weights, weight_grad))
-    q = jnp.transpose(queries.reshape(tok, groups, width), (1, 0, 2))
-    ks = jnp.transpose(sub_keys.reshape(rows, groups, width), (1, 0, 2))
     vmem = pl.BlockSpec(memory_space=pltpu.VMEM)
     key_grad, in_grad = pl.pallas_call(
         kernel,
@@ -283,9 +316,17 @@
             jax.ShapeDtypeStruct((groups, 16, width), F32),
             jax.ShapeDtypeStruct((tok // 4, model), BF16),
         ),
-        in_specs=[vmem] * 6 + [pl.BlockSpec(memory_space=pl.ANY)],
+        in_specs=[pl.BlockSpec(memory_space=pltpu.HBM)] * 7,
         out_specs=(vmem, vmem),
         scratch_shapes=[
+            pltpu.VMEM(idx.shape, idx.dtype),
+            pltpu.VMEM(pair.shape, pair.dtype),
+            pltpu.VMEM(w.shape, w.dtype),
+            pltpu.VMEM(wg.shape, wg.dtype),
+            pltpu.VMEM(queries.shape, queries.dtype),
+            pltpu.VMEM(sub_keys.shape, sub_keys.dtype),
+            pltpu.VMEM((groups, tok, width), queries.dtype),
+            pltpu.VMEM((groups, rows, width), sub_keys.dtype),
             pltpu.VMEM((groups, topk, tok), F32),
             pltpu.VMEM((groups, topk, tok), F32),
             pltpu.VMEM((topk, tok), F32),
@@ -296,6 +337,7 @@
             pltpu.VMEM((3, groups, rows, width), BF16),
             pltpu.VMEM((model, groups * width), BF16),
             pltpu.VMEM((tok, groups * width), BF16),
+            pltpu.VMEM((groups, tok, width), F32),
             pltpu.VMEM((groups, 3, 4, 64, width), BF16),
             pltpu.VMEM((groups, 4, 64, width), BF16),
             pltpu.VMEM((groups, 4, 64, width), BF16),
@@ -308,13 +350,14 @@
             pltpu.VMEM((CHUNKS, 64, wide), BF16),
             pltpu.VMEM((CHUNKS, 64, wide), BF16),
             pltpu.SemaphoreType.DMA((CHUNKS,)),
+            pltpu.SemaphoreType.DMA((6,)),
             pltpu.SemaphoreType.DMA((MESSAGES,)),
             pltpu.SemaphoreType.DMA((MESSAGES,)),
         ],
         compiler_params=pltpu.CompilerParams(
             collective_id=0, has_side_effects=True, vmem_limit_bytes=48 * 2**20
         ),
-    )(idx, pair, w, wg, q, ks, query_weight)
+    )(idx, pair, w, wg, queries, sub_keys, query_weight)
     sub_key_grad = jnp.transpose(key_grad, (1, 0, 2)).reshape(16, heads, halves, width)
     return sub_key_grad, in_grad
 

time: 61.8 us -> 63.6 us (1.029)
  Pallas kernels: 53.7 us -> 55.7 us
    pallas_call x1, Pallas kernels: 53.7 us -> 55.7 us  [on_device(): pl.pallas_call(kernel, out_shape=(jax.ShapeDtypeStruct((groups, 16, width...]
    unnamed x12 -> x14, local copies, waits for them, and re-layouts: 7.12 us -> 6.97 us
where the time goes in v2:
time: 63.6 us; the launch traced here: 63.3 us
  Pallas kernels  55.7 us (88%)
  local copies, waits for them, and re-layouts  6.97 us (11%)
  between operations  0.65 us (1%)
    pallas_call x1, Pallas kernels, on_device(): pl.pallas_call(kernel, out_shape=(jax.ShapeDtypeStruct((groups, 16, width...  55.7 us
    unnamed x14, local copies, waits for them, and re-layouts  6.97 us

profile of v2, /device:TPU:1, one launch (start us, length us, event | category | flops | bytes accessed | tf_op | source)
XLA Modules:
  0.0 63.3 jit_solution(8864514936195455716)
XLA Ops:
  0.6 0.0 copy-start
  0.6 1.0 %copy-done = bf16[256,2,2,256]{3,2,1,0:T(2,128)(2,1)S(1)} copy-done((bf16[256,2,2,256]{3,2,1,0:T(2,128)(2,1)S(1)}, bf16[256,2,2,256]{3,2,1,0:T(2,128)(2,1)}, u32[]{:S(2)}) %copy-start) | copy-done | bytes 524312
  1.7 0.0 copy-start.1
  1.7 1.0 %copy-done.1 = bf16[256,2,2,256]{3,2,1,0:T(2,128)(2,1)S(1)} copy-done((bf16[256,2,2,256]{3,2,1,0:T(2,128)(2,1)S(1)}, bf16[256,2,2,256]{3,2,1,0:T(2,128)(2,1)}, u32[]{:S(2)}) %copy-start.1) | copy-done | bytes 524312
  2.7 0.0 copy-start.2
  2.7 0.9 %copy-done.2 = s32[256,2,2,32]{0,3,2,1:T(8,128)S(1)} copy-done((s32[256,2,2,32]{0,3,2,1:T(8,128)S(1)}, s32[256,2,2,32]{0,3,2,1:T(8,128)}, u32[]{:S(2)}) %copy-start.2) | copy-done | bytes 131096
  3.6 0.0 copy-start.3
  3.6 0.8 %copy-done.3 = s32[256,2,32]{0,2,1:T(8,128)S(1)} copy-done((s32[256,2,32]{0,2,1:T(8,128)S(1)}, s32[256,2,32]{0,2,1:T(8,128)}, u32[]{:S(2)}) %copy-start.3) | copy-done | bytes 65560
  4.5 0.0 copy-start.4
  4.5 0.8 %copy-done.4 = f32[256,2,32]{0,2,1:T(8,128)S(1)} copy-done((f32[256,2,32]{0,2,1:T(8,128)S(1)}, f32[256,2,32]{0,2,1:T(8,128)}, u32[]{:S(2)}) %copy-start.4) | copy-done | bytes 65560
  5.3 0.0 copy-start.5
  5.3 0.8 %copy-done.5 = f32[256,2,32]{0,2,1:T(8,128)S(1)} copy-done((f32[256,2,32]{0,2,1:T(8,128)S(1)}, f32[256,2,32]{0,2,1:T(8,128)}, u32[]{:S(2)}) %copy-start.5) | copy-done | bytes 65560
  6.1 55.7 %shard_map.86 = (f32[4,16,256]{2,1,0:T(8,128)S(1)}, bf16[64,4096]{1,0:T(8,128)(2,1)S(1)}) custom-call(s32[4,32,256]{2,1,0:T(8,128)S(1)} %bitcast.9, s32[2,32,256]{2,1,0:T(8,128)S(1)} %bitcast.10, f32[2,32,256]{2,1,0:T(8,128)S(1)} %bitcast.11, f32[2,32,256]{2,1,0:T(8,128)S(1)} %bitcast.12, bf16[256,2,2,256]{3,2,1,0:T(2,128)(2,1)S(1)} %copy-done, ...), custom_call_target="tpu_custom_call" | custom-call | tf_op jit(solution)/shard_map/pallas_call | solution.py:313
  61.8 0.7 %copy.9 = f32[16,2,2,256]{3,2,1,0:T(2,128)} copy(f32[16,2,2,256]{3,0,2,1:T(8,128)S(1)} %bitcast.13) | data formatting | bytes 131072
  62.5 0.8 %copy.11 = bf16[64,4096]{1,0:T(8,128)(2,1)} copy(bf16[64,4096]{1,0:T(8,128)(2,1)S(1)} %get-tuple-element.11) | data formatting | bytes 1048576
Async XLA Ops:
  0.6 1.0 %copy-start = (bf16[256,2,2,256]{3,2,1,0:T(2,128)(2,1)S(1)}, bf16[256,2,2,256]{3,2,1,0:T(2,128)(2,1)}, u32[]{:S(2)}) copy-start(bf16[256,2,2,256]{3,2,1,0:T(2,128)(2,1)} %q_hbm.1) | copy-start | bytes 1572868
  1.7 1.0 %copy-start.1 = (bf16[256,2,2,256]{3,2,1,0:T(2,128)(2,1)S(1)}, bf16[256,2,2,256]{3,2,1,0:T(2,128)(2,1)}, u32[]{:S(2)}) copy-start(bf16[256,2,2,256]{3,2,1,0:T(2,128)(2,1)} %ks_hbm.1) | copy-start | bytes 1572868
  2.7 0.9 %copy-start.2 = (s32[256,2,2,32]{0,3,2,1:T(8,128)S(1)}, s32[256,2,2,32]{0,3,2,1:T(8,128)}, u32[]{:S(2)}) copy-start(s32[256,2,2,32]{0,3,2,1:T(8,128)} %param.10) | copy-start | bytes 393220
  3.6 0.8 %copy-start.3 = (s32[256,2,32]{0,2,1:T(8,128)S(1)}, s32[256,2,32]{0,2,1:T(8,128)}, u32[]{:S(2)}) copy-start(s32[256,2,32]{0,2,1:T(8,128)} %param.11) | copy-start | bytes 196612
  4.5 0.8 %copy-start.4 = (f32[256,2,32]{0,2,1:T(8,128)S(1)}, f32[256,2,32]{0,2,1:T(8,128)}, u32[]{:S(2)}) copy-start(f32[256,2,32]{0,2,1:T(8,128)} %param.12) | copy-start | bytes 196612
  5.3 0.8 %copy-start.5 = (f32[256,2,32]{0,2,1:T(8,128)S(1)}, f32[256,2,32]{0,2,1:T(8,128)}, u32[]{:S(2)}) copy-start(f32[256,2,32]{0,2,1:T(8,128)} %param.13) | copy-start | bytes 196612

commit v3 on v2

--- a/solution.py
+++ b/solution.py
@@ -15,6 +15,7 @@
 F32 = jnp.float32
 BF16 = jnp.bfloat16
 CHUNKS = 8
+OTHERS = (2, 1, -1)
 MESSAGES = 96
 
 
@@ -23,7 +24,7 @@
     key_out, in_out,
     idx_ref, pair_ref, w_ref, wg_ref, q_raw, ks_raw, q_ref, ks_ref,
     idxf, val, score, first, second, table, part, kbuf, wv, qg, qsum,
-    r1, s3, res1, r2, s23, res2, r3, po, c1, c2s, c2r,
+    r1, s3, res1, r2, res2, r3, po, c1, c2s, c2r,
     w_sem, in_sem, send_sem, recv_sem,
 ):
     y, x, k, t = (lax.axis_index(a) for a in AXES)
@@ -40,8 +41,8 @@
     other_chip = {"tensor": (1 - zl) * 2 + c}
 
     barrier = pltpu.get_barrier_semaphore()
-    partners = [near(a, s) for a in ("dp_0", "dp_1") for s in (1, -1)]
-    partners += [near("key", s) for s in (1, -1, 2)] + [other_core, other_chip]
+    partners = [near(a, s) for a in ("dp_0", "dp_1") for s in OTHERS]
+    partners += [near("key", s) for s in OTHERS] + [other_core, other_chip]
     for device in partners:
         pl.semaphore_signal(barrier, inc=1, device_id=device, device_id_type=MESH)
 
@@ -108,24 +109,17 @@
             arrived(("z1", slot, hx), piece)
             send(("z2", hx), piece, kbuf.at[2, hx, quarter(hx)], near("key", d))
 
-    def share_first(slot, hx, name=None):
+    def share(slot, hx, name=None):
         piece = kbuf.at[slot, hx, quarter(hx)]
         if name is not None:
             arrived(name, piece)
-        for d in (way(hx), -way(hx)):
-            send(("g1", slot, hx, d), piece, piece, near(ring(hx), d))
-
-    def share_second(slot, hx):
-        d = way(hx)
-        piece = kbuf.at[slot, hx, quarter(hx, -d)]
-        arrived(("g1", slot, hx, d), piece)
-        send(("g2", slot, hx), piece, piece, near(ring(hx), d))
+        for step in OTHERS:
+            send(("g", slot, hx, step), piece, piece, near(ring(hx), step))
 
     def share_end(slot):
         for hx in range(4):
-            d = way(hx)
-            arrived(("g1", slot, hx, -d), kbuf.at[slot, hx, quarter(hx, d)])
-            arrived(("g2", slot, hx), kbuf.at[slot, hx, quarter(hx, 2)])
+            for step in OTHERS:
+                arrived(("g", slot, hx, step), kbuf.at[slot, hx, quarter(hx, -step)])
 
     def early(hx):
         return (1 - way(hx)) // 2
@@ -193,55 +187,54 @@
         return "dp_1" if (hx < 2) == (stage == 1) else "dp_0"
 
     into = {1: r1, 2: r2}
-    staged = {1: s3, 2: s23}
+
+    def relayed(stage, hx):
+        return stage == 1 and hx % 2 == 0
 
     def reduce_first(stage, hx):
-        axis, d = axis_of(stage, hx), way(hx)
-        send((stage, hx, 0), block(stage, hx, 2), into[stage].at[hx, 0], near(axis, d))
-        send((stage, hx, 1), block(stage, hx, -d), into[stage].at[hx, 1], near(axis, -d))
+        axis, got = axis_of(stage, hx), into[stage]
+        if relayed(stage, hx):
+            send((stage, hx, 0), block(stage, hx, 2), got.at[hx, 0], near(axis, 1))
+            send((stage, hx, 2), block(stage, hx, -1), got.at[hx, 2], near(axis, -1))
+        else:
+            for n, step in enumerate(OTHERS):
+                send((stage, hx, n), block(stage, hx, step), got.at[hx, n], near(axis, step))
 
     def reduce_second(stage, hx):
-        axis, d = axis_of(stage, hx), way(hx)
-        arrived((stage, hx, 0), into[stage].at[hx, 0])
-        both = block(stage, hx, d)[...].astype(F32) + into[stage][hx, 0].astype(F32)
-        staged[stage][hx] = both.astype(BF16)
-        send((stage, hx, 2), staged[stage].at[hx], into[stage].at[hx, 2], near(axis, d))
+        axis, got = axis_of(stage, hx), into[stage]
+        arrived((stage, hx, 0), got.at[hx, 0])
+        both = block(stage, hx, 1)[...].astype(F32) + got[hx, 0].astype(F32)
+        s3[hx] = both.astype(BF16)
+        send((stage, hx, 1), s3.at[hx], got.at[hx, 1], near(axis, 1))
 
     def reduce_end(stage, hx):
         got = into[stage]
-        arrived((stage, hx, 1), got.at[hx, 1])
-        arrived((stage, hx, 2), got.at[hx, 2])
-        total = block(stage, hx, 0)[...].astype(F32) + got[hx, 1].astype(F32) + got[hx, 2].astype(F32)
+        total = block(stage, hx, 0)[...].astype(F32)
+        for n in range(1 if relayed(stage, hx) else 0, 3):
+            arrived((stage, hx, n), got.at[hx, n])
+            total = total + got[hx, n].astype(F32)
         if stage == 1:
             res1[hx] = total.astype(BF16)
         else:
             res2[:, hx] = total.astype(BF16).reshape(4, 16, total.shape[-1])
 
-    key_steps = (1, -1, 2)
-
     build(0)
     reduce_first(1, 0)
     key_second()
     for hx in range(4):
-        share_first(early(hx), hx)
+        share(early(hx), hx)
     build(2)
     reduce_first(1, 2)
     for hx in range(4):
-        share_first(1 - early(hx), hx, ("z1", 1 - early(hx), hx))
+        share(1 - early(hx), hx, ("z1", 1 - early(hx), hx))
     build(1)
+    reduce_second(1, 0)
+    for hx in range(4):
+        share(2, hx, ("z2", hx))
     reduce_first(1, 1)
-    for hx in range(4):
-        share_second(early(hx), hx)
-    for hx in (0, 2):
-        reduce_second(1, hx)
-    for hx in range(4):
-        share_first(2, hx, ("z2", hx))
-    for hx in range(4):
-        share_second(1 - early(hx), hx)
     build(3)
+    reduce_second(1, 2)
     reduce_first(1, 3)
-    for hx in range(4):
-        share_second(2, hx)
     share_end(0)
     share_end(1)
 
@@ -252,7 +245,6 @@
 
     for hx in range(4):
         qsum[hx] = shard_term(hx, 0, ks_ref[hx]) + shard_term(hx, -1, kbuf[0, hx]) + shard_term(hx, 1, kbuf[1, hx])
-    reduce_second(1, 1)
     share_end(2)
     for hx in range(4):
         total = qsum[hx] + shard_term(hx, 2, kbuf[2, hx])
@@ -269,28 +261,32 @@
         c2s[j] = (po[j, 1 - zl, c].astype(F32) + c1[j, 1 - zl].astype(F32)).astype(BF16)
         send(("c2", j), c2s.at[j], c2r.at[j], other_chip)
 
+    def finish(j):
+        arrived(("c2", j), c2r.at[j])
+        total = po[j, zl, c].astype(F32) + c1[j, zl].astype(F32) + c2r[j].astype(F32)
+        in_out[:, j * wide : (j + 1) * wide] = total.astype(BF16)
+
+    held = 2
     for j in range(CHUNKS):
         project(j)
         if j >= 2:
             pass_on(j - 2)
-        if j == 2:
-            reduce_second(1, 3)
-        if j >= CHUNKS - 4:
-            hx = (0, 2, 1, 3)[j - CHUNKS + 4]
-            reduce_end(1, hx)
-            reduce_first(2, hx)
-    pass_on(CHUNKS - 2)
-    pass_on(CHUNKS - 1)
-    for hx in (0, 2, 1, 3):
-        reduce_second(2, hx)
+        if j in (2, 3):
+            reduce_end(1, 2 * j - 4)
+            reduce_first(2, 2 * j - 4)
+    for hx in (1, 3):
+        reduce_end(1, hx)
+        reduce_first(2, hx)
+    for j in range(2):
+        finish(j)
     for hx in (0, 2, 1, 3):
         reduce_end(2, hx)
-    for n, step in enumerate(key_steps):
+    for n, step in enumerate(OTHERS):
         send((3, n), res2.at[at("key", step)], r3.at[n], near("key", step))
-    for j in range(CHUNKS):
-        arrived(("c2", j), c2r.at[j])
-        total = po[j, zl, c].astype(F32) + c1[j, zl].astype(F32) + c2r[j].astype(F32)
-        in_out[:, j * wide : (j + 1) * wide] = total.astype(BF16)
+    for j in range(CHUNKS - held, CHUNKS):
+        pass_on(j)
+    for j in range(2, CHUNKS):
+        finish(j)
     total = res2[k].astype(F32)
     for n in range(3):
         arrived((3, n), r3.at[n])
@@ -342,7 +338,6 @@
             pltpu.VMEM((groups, 4, 64, width), BF16),
             pltpu.VMEM((groups, 4, 64, width), BF16),
             pltpu.VMEM((groups, 3, 64, width), BF16),
-            pltpu.VMEM((groups, 64, width), BF16),
             pltpu.VMEM((4, groups, 16, width), BF16),
             pltpu.VMEM((3, groups, 16, width), BF16),
             pltpu.VMEM((CHUNKS, 2, 2, 64, wide), BF16),
@@ -355,9 +350,9 @@
             pltpu.SemaphoreType.DMA((MESSAGES,)),
         ],
         compiler_params=pltpu.CompilerParams(
-            collective_id=0, has_side_effects=True, vmem_limit_bytes=48 * 2**20
+            collective_id=0, has_side_effects=True, vmem_limit_bytes=40000000
         ),
-    )(idx, pair, w, wg, queries, sub_keys, query_weight)
+    )(*(pltpu.with_memory_space_constraint(v, pltpu.HBM) for v in (idx, pair, w, wg, queries, sub_keys, query_weight)))
     sub_key_grad = jnp.transpose(key_grad, (1, 0, 2)).reshape(16, heads, halves, width)
     return sub_key_grad, in_grad
 

time: 63.6 us -> 54.8 us (0.86)
  local copies, waits for them, and re-layouts: 6.97 us -> 1.47 us
  Pallas kernels: 55.7 us -> 52.6 us
    unnamed x14 -> x2, local copies, waits for them, and re-layouts: 6.97 us -> 1.47 us
    pallas_call x1, Pallas kernels: 55.7 us -> 52.6 us  [on_device(): pl.pallas_call(kernel, out_shape=(jax.ShapeDtypeStruct((groups, 16, width...]
where the time goes in v3:
time: 54.8 us; the launch traced here: 54.7 us
  Pallas kernels  52.6 us (96%)
  local copies, waits for them, and re-layouts  1.47 us (3%)
  between operations  0.64 us (1%)
    pallas_call x1, Pallas kernels, on_device(): pl.pallas_call(kernel, out_shape=(jax.ShapeDtypeStruct((groups, 16, width...  52.6 us
    unnamed x2, local copies, waits for them, and re-layouts  1.47 us

profile of v3, /device:TPU:1, one launch (start us, length us, event | category | flops | bytes accessed | tf_op | source)
XLA Modules:
  0.0 54.7 jit_solution(12058418197245666414)
XLA Ops:
  0.6 52.6 %shard_map.86 = (f32[4,16,256]{2,1,0:T(8,128)S(1)}, bf16[64,4096]{1,0:T(8,128)(2,1)S(1)}) custom-call(s32[4,32,256]{2,1,0:T(8,128)} %bitcast.10, s32[2,32,256]{2,1,0:T(8,128)} %bitcast.11, f32[2,32,256]{2,1,0:T(8,128)} %bitcast.12, f32[2,32,256]{2,1,0:T(8,128)} %bitcast.13, bf16[256,2,2,256]{3,2,1,0:T(2,128)(2,1)} %q_hbm.1, bf16[256,2,2,256]{3,2,1,0:T(2,128)(2,1)} %ks_hbm.1, ...), custom_call_target="tpu_custom_call" | custom-call | tf_op jit(solution)/shard_map/pallas_call | solution.py:309
  53.3 0.7 %copy.9 = f32[16,2,2,256]{3,2,1,0:T(2,128)} copy(f32[16,2,2,256]{3,0,2,1:T(8,128)S(1)} %bitcast.9) | data formatting | bytes 131072
  54.0 0.8 %copy.11 = bf16[64,4096]{1,0:T(8,128)(2,1)} copy(bf16[64,4096]{1,0:T(8,128)(2,1)S(1)} %get-tuple-element.11) | data formatting | bytes 1048576

commit v4 on v3

--- a/solution.py
+++ b/solution.py
@@ -22,7 +22,7 @@
 def kernel(
     idx_hbm, pair_hbm, w_hbm, wg_hbm, q_hbm, ks_hbm, wq_ref,
     key_out, in_out,
-    idx_ref, pair_ref, w_ref, wg_ref, q_raw, ks_raw, q_ref, ks_ref,
+    idx_ref, pair_ref, w_ref, wg_ref, q_raw, ks_raw, pairs, q_ref, ks_ref,
     idxf, val, score, first, second, table, part, kbuf, wv, qg, qsum,
     r1, s3, res1, r2, res2, r3, po, c1, c2s, c2r,
     w_sem, in_sem, send_sem, recv_sem,
@@ -63,8 +63,17 @@
     for load in loads:
         load.start()
     fetched[0].wait()
-    for hx in range(4):
-        ks_ref[hx] = ks_raw[:, hx // 2, hx % 2, :]
+
+    def lay_out(raw, dst):
+        for h in range(2):
+            both = raw[:, h].astype(F32).reshape(2 * raw.shape[0], raw.shape[3])
+            for n in range(raw.shape[3] // 128):
+                lanes = slice(n * 128, (n + 1) * 128)
+                pairs[n] = both[:, lanes]
+                for half in range(2):
+                    dst[2 * h + half, :, lanes] = pairs[n, pl.ds(half, raw.shape[0], stride=2), :].astype(BF16)
+
+    lay_out(ks_raw, ks_ref)
     pl.semaphore_wait(barrier, len(partners))
 
     names, sent = {}, []
@@ -129,8 +138,7 @@
 
     for one in fetched[1:]:
         one.wait()
-    for hx in range(4):
-        q_ref[hx] = q_raw[:, hx // 2, hx % 2, :]
+    lay_out(q_raw, q_ref)
 
     kept, tokens = idx_ref.shape[1], idx_ref.shape[2]
     for hx in range(4):
@@ -187,6 +195,7 @@
         return "dp_1" if (hx < 2) == (stage == 1) else "dp_0"
 
     into = {1: r1, 2: r2}
+    lean = 1 - 2 * c
 
     def relayed(stage, hx):
         return stage == 1 and hx % 2 == 0
@@ -194,8 +203,8 @@
     def reduce_first(stage, hx):
         axis, got = axis_of(stage, hx), into[stage]
         if relayed(stage, hx):
-            send((stage, hx, 0), block(stage, hx, 2), got.at[hx, 0], near(axis, 1))
-            send((stage, hx, 2), block(stage, hx, -1), got.at[hx, 2], near(axis, -1))
+            send((stage, hx, 0), block(stage, hx, 2), got.at[hx, 0], near(axis, lean))
+            send((stage, hx, 2), block(stage, hx, -lean), got.at[hx, 2], near(axis, -lean))
         else:
             for n, step in enumerate(OTHERS):
                 send((stage, hx, n), block(stage, hx, step), got.at[hx, n], near(axis, step))
@@ -203,9 +212,9 @@
     def reduce_second(stage, hx):
         axis, got = axis_of(stage, hx), into[stage]
         arrived((stage, hx, 0), got.at[hx, 0])
-        both = block(stage, hx, 1)[...].astype(F32) + got[hx, 0].astype(F32)
+        both = block(stage, hx, lean)[...].astype(F32) + got[hx, 0].astype(F32)
         s3[hx] = both.astype(BF16)
-        send((stage, hx, 1), s3.at[hx], got.at[hx, 1], near(axis, 1))
+        send((stage, hx, 1), s3.at[hx], got.at[hx, 1], near(axis, lean))
 
     def reduce_end(stage, hx):
         got = into[stage]
@@ -220,20 +229,20 @@
 
     build(0)
     reduce_first(1, 0)
-    key_second()
-    for hx in range(4):
-        share(early(hx), hx)
     build(2)
     reduce_first(1, 2)
+    key_second()
+    for hx in range(4):
+        share(early(hx), hx)
+    build(1)
     for hx in range(4):
         share(1 - early(hx), hx, ("z1", 1 - early(hx), hx))
-    build(1)
+    build(3)
+    for hx in range(4):
+        share(2, hx, ("z2", hx))
     reduce_second(1, 0)
-    for hx in range(4):
-        share(2, hx, ("z2", hx))
+    reduce_second(1, 2)
     reduce_first(1, 1)
-    build(3)
-    reduce_second(1, 2)
     reduce_first(1, 3)
     share_end(0)
     share_end(1)
@@ -321,6 +330,7 @@
             pltpu.VMEM(wg.shape, wg.dtype),
             pltpu.VMEM(queries.shape, queries.dtype),
             pltpu.VMEM(sub_keys.shape, sub_keys.dtype),
+            pltpu.VMEM((width // 128, 2 * tok, 128), F32),
             pltpu.VMEM((groups, tok, width), queries.dtype),
             pltpu.VMEM((groups, rows, width), sub_keys.dtype),
             pltpu.VMEM((groups, topk, tok), F32),

time: 54.8 us -> 52.7 us (0.962)
  Pallas kernels: 52.6 us -> 50.5 us
    pallas_call x1, Pallas kernels: 52.6 us -> 50.5 us  [on_device(): pl.pallas_call(kernel, out_shape=(jax.ShapeDtypeStruct((groups, 16, width...]
where the time goes in v4:
time: 52.7 us; the launch traced here: 52.6 us
  Pallas kernels  50.5 us (96%)
  local copies, waits for them, and re-layouts  1.47 us (3%)
  between operations  0.64 us (1%)
    pallas_call x1, Pallas kernels, on_device(): pl.pallas_call(kernel, out_shape=(jax.ShapeDtypeStruct((groups, 16, width...  50.5 us
    unnamed x2, local copies, waits for them, and re-layouts  1.47 us

profile of v4, /device:TPU:1, one launch (start us, length us, event | category | flops | bytes accessed | tf_op | source)
XLA Modules:
  0.0 52.6 jit_solution(12174245094330708325)
XLA Ops:
  0.6 50.5 %shard_map.86 = (f32[4,16,256]{2,1,0:T(8,128)S(1)}, bf16[64,4096]{1,0:T(8,128)(2,1)S(1)}) custom-call(s32[4,32,256]{2,1,0:T(8,128)} %bitcast.10, s32[2,32,256]{2,1,0:T(8,128)} %bitcast.11, f32[2,32,256]{2,1,0:T(8,128)} %bitcast.12, f32[2,32,256]{2,1,0:T(8,128)} %bitcast.13, bf16[256,2,2,256]{3,2,1,0:T(2,128)(2,1)} %q_hbm.1, bf16[256,2,2,256]{3,2,1,0:T(2,128)(2,1)} %ks_hbm.1, ...), custom_call_target="tpu_custom_call" | custom-call | tf_op jit(solution)/shard_map/pallas_call | solution.py:318
  51.1 0.7 %copy.9 = f32[16,2,2,256]{3,2,1,0:T(2,128)} copy(f32[16,2,2,256]{3,0,2,1:T(8,128)S(1)} %bitcast.9) | data formatting | bytes 131072
  51.8 0.8 %copy.11 = bf16[64,4096]{1,0:T(8,128)(2,1)} copy(bf16[64,4096]{1,0:T(8,128)(2,1)S(1)} %get-tuple-element.11) | data formatting | bytes 1048576

commit v5 on v4

--- a/solution.py
+++ b/solution.py
@@ -122,13 +122,20 @@
         piece = kbuf.at[slot, hx, quarter(hx)]
         if name is not None:
             arrived(name, piece)
-        for step in OTHERS:
+        for step in OTHERS if slot == 2 else (1, -1):
             send(("g", slot, hx, step), piece, piece, near(ring(hx), step))
+
+    def share_second(slot, hx):
+        d = way(hx)
+        piece = kbuf.at[slot, hx, quarter(hx, -d)]
+        arrived(("g", slot, hx, d), piece)
+        send(("g", slot, hx, 2), piece, piece, near(ring(hx), d))
 
     def share_end(slot):
         for hx in range(4):
             for step in OTHERS:
-                arrived(("g", slot, hx, step), kbuf.at[slot, hx, quarter(hx, -step)])
+                if slot == 2 or step != way(hx):
+                    arrived(("g", slot, hx, step), kbuf.at[slot, hx, quarter(hx, -step)])
 
     def early(hx):
         return (1 - way(hx)) // 2
@@ -225,7 +232,7 @@
         if stage == 1:
             res1[hx] = total.astype(BF16)
         else:
-            res2[:, hx] = total.astype(BF16).reshape(4, 16, total.shape[-1])
+            res2[:, hx % 2 * 2 + hx // 2] = total.astype(BF16).reshape(4, 16, total.shape[-1])
 
     build(0)
     reduce_first(1, 0)
@@ -240,8 +247,12 @@
     build(3)
     for hx in range(4):
         share(2, hx, ("z2", hx))
+    for hx in range(4):
+        share_second(early(hx), hx)
     reduce_second(1, 0)
     reduce_second(1, 2)
+    for hx in range(4):
+        share_second(1 - early(hx), hx)
     reduce_first(1, 1)
     reduce_first(1, 3)
     share_end(0)
@@ -275,7 +286,11 @@
         total = po[j, zl, c].astype(F32) + c1[j, zl].astype(F32) + c2r[j].astype(F32)
         in_out[:, j * wide : (j + 1) * wide] = total.astype(BF16)
 
-    held = 2
+    def key_send(part):
+        here = pl.ds(2 * part, 2)
+        for n, step in enumerate(OTHERS):
+            send((3, part, n), res2.at[at("key", step), here], r3.at[n, here], near("key", step))
+
     for j in range(CHUNKS):
         project(j)
         if j >= 2:
@@ -286,21 +301,21 @@
     for hx in (1, 3):
         reduce_end(1, hx)
         reduce_first(2, hx)
-    for j in range(2):
+        pass_on(CHUNKS - 2 + hx // 2)
+    for part in range(2):
+        for hx in (part, part + 2):
+            reduce_end(2, hx)
+        key_send(part)
+    for j in range(CHUNKS):
         finish(j)
-    for hx in (0, 2, 1, 3):
-        reduce_end(2, hx)
-    for n, step in enumerate(OTHERS):
-        send((3, n), res2.at[at("key", step)], r3.at[n], near("key", step))
-    for j in range(CHUNKS - held, CHUNKS):
-        pass_on(j)
-    for j in range(2, CHUNKS):
-        finish(j)
-    total = res2[k].astype(F32)
-    for n in range(3):
-        arrived((3, n), r3.at[n])
-        total = total + r3[n].astype(F32)
-    key_out[...] = total
+    for part in range(2):
+        here = pl.ds(2 * part, 2)
+        total = res2[k, here].astype(F32)
+        for n in range(3):
+            arrived((3, part, n), r3.at[n, here])
+            total = total + r3[n, here].astype(F32)
+        for n in range(2):
+            key_out[part + 2 * n] = total[n]
     for one in sent:
         one.wait_send()
 

time: 52.7 us -> 56.8 us (1.078)
  Pallas kernels: 50.5 us -> 54.6 us
    pallas_call x1, Pallas kernels: 50.5 us -> 54.6 us  [on_device(): pl.pallas_call(kernel, out_shape=(jax.ShapeDtypeStruct((groups, 16, width...]
where the time goes in v5:
time: 56.8 us; the launch traced here: 56.7 us
  Pallas kernels  54.6 us (96%)
  local copies, waits for them, and re-layouts  1.47 us (3%)
  between operations  0.64 us (1%)
    pallas_call x1, Pallas kernels, on_device(): pl.pallas_call(kernel, out_shape=(jax.ShapeDtypeStruct((groups, 16, width...  54.6 us
    unnamed x2, local copies, waits for them, and re-layouts  1.47 us

profile of v5, /device:TPU:1, one launch (start us, length us, event | category | flops | bytes accessed | tf_op | source)
XLA Modules:
  0.0 56.7 jit_solution(14986011143533881020)
XLA Ops:
  0.6 54.6 %shard_map.86 = (f32[4,16,256]{2,1,0:T(8,128)S(1)}, bf16[64,4096]{1,0:T(8,128)(2,1)S(1)}) custom-call(s32[4,32,256]{2,1,0:T(8,128)} %bitcast.10, s32[2,32,256]{2,1,0:T(8,128)} %bitcast.11, f32[2,32,256]{2,1,0:T(8,128)} %bitcast.12, f32[2,32,256]{2,1,0:T(8,128)} %bitcast.13, bf16[256,2,2,256]{3,2,1,0:T(2,128)(2,1)} %q_hbm.1, bf16[256,2,2,256]{3,2,1,0:T(2,128)(2,1)} %ks_hbm.1, ...), custom_call_target="tpu_custom_call" | custom-call | tf_op jit(solution)/shard_map/pallas_call | solution.py:333
  55.2 0.7 %copy.9 = f32[16,2,2,256]{3,2,1,0:T(2,128)} copy(f32[16,2,2,256]{3,0,2,1:T(8,128)S(1)} %bitcast.9) | data formatting | bytes 131072
  55.9 0.8 %copy.11 = bf16[64,4096]{1,0:T(8,128)(2,1)} copy(bf16[64,4096]{1,0:T(8,128)(2,1)S(1)} %get-tuple-element.11) | data formatting | bytes 1048576

commit v6 on v5

--- a/solution.py
+++ b/solution.py
@@ -122,20 +122,13 @@
         piece = kbuf.at[slot, hx, quarter(hx)]
         if name is not None:
             arrived(name, piece)
-        for step in OTHERS if slot == 2 else (1, -1):
+        for step in OTHERS:
             send(("g", slot, hx, step), piece, piece, near(ring(hx), step))
-
-    def share_second(slot, hx):
-        d = way(hx)
-        piece = kbuf.at[slot, hx, quarter(hx, -d)]
-        arrived(("g", slot, hx, d), piece)
-        send(("g", slot, hx, 2), piece, piece, near(ring(hx), d))
 
     def share_end(slot):
         for hx in range(4):
             for step in OTHERS:
-                if slot == 2 or step != way(hx):
-                    arrived(("g", slot, hx, step), kbuf.at[slot, hx, quarter(hx, -step)])
+                arrived(("g", slot, hx, step), kbuf.at[slot, hx, quarter(hx, -step)])
 
     def early(hx):
         return (1 - way(hx)) // 2
@@ -247,12 +240,8 @@
     build(3)
     for hx in range(4):
         share(2, hx, ("z2", hx))
-    for hx in range(4):
-        share_second(early(hx), hx)
     reduce_second(1, 0)
     reduce_second(1, 2)
-    for hx in range(4):
-        share_second(1 - early(hx), hx)
     reduce_first(1, 1)
     reduce_first(1, 3)
     share_end(0)

time: 56.8 us -> 54.4 us (0.958)
  Pallas kernels: 54.6 us -> 52.2 us
    pallas_call x1, Pallas kernels: 54.6 us -> 52.2 us  [on_device(): pl.pallas_call(kernel, out_shape=(jax.ShapeDtypeStruct((groups, 16, width...]
where the time goes in v6:
time: 54.4 us; the launch traced here: 54.3 us
  Pallas kernels  52.2 us (96%)
  local copies, waits for them, and re-layouts  1.47 us (3%)
  between operations  0.64 us (1%)
    pallas_call x1, Pallas kernels, on_device(): pl.pallas_call(kernel, out_shape=(jax.ShapeDtypeStruct((groups, 16, width...  52.2 us
    unnamed x2, local copies, waits for them, and re-layouts  1.47 us

profile of v6, /device:TPU:1, one launch (start us, length us, event | category | flops | bytes accessed | tf_op | source)
XLA Modules:
  0.0 54.3 jit_solution(7867572049502200138)
XLA Ops:
  0.6 52.2 %shard_map.86 = (f32[4,16,256]{2,1,0:T(8,128)S(1)}, bf16[64,4096]{1,0:T(8,128)(2,1)S(1)}) custom-call(s32[4,32,256]{2,1,0:T(8,128)} %bitcast.10, s32[2,32,256]{2,1,0:T(8,128)} %bitcast.11, f32[2,32,256]{2,1,0:T(8,128)} %bitcast.12, f32[2,32,256]{2,1,0:T(8,128)} %bitcast.13, bf16[256,2,2,256]{3,2,1,0:T(2,128)(2,1)} %q_hbm.1, bf16[256,2,2,256]{3,2,1,0:T(2,128)(2,1)} %ks_hbm.1, ...), custom_call_target="tpu_custom_call" | custom-call | tf_op jit(solution)/shard_map/pallas_call | solution.py:322
  52.8 0.7 %copy.9 = f32[16,2,2,256]{3,2,1,0:T(2,128)} copy(f32[16,2,2,256]{3,0,2,1:T(8,128)S(1)} %bitcast.9) | data formatting | bytes 131072
  53.5 0.8 %copy.11 = bf16[64,4096]{1,0:T(8,128)(2,1)} copy(bf16[64,4096]{1,0:T(8,128)(2,1)S(1)} %get-tuple-element.11) | data formatting | bytes 1048576

commit v7 on v6

--- a/solution.py
+++ b/solution.py
@@ -282,7 +282,7 @@
 
     for j in range(CHUNKS):
         project(j)
-        if j >= 2:
+        if 2 <= j < CHUNKS - 2:
             pass_on(j - 2)
         if j in (2, 3):
             reduce_end(1, 2 * j - 4)
@@ -290,11 +290,12 @@
     for hx in (1, 3):
         reduce_end(1, hx)
         reduce_first(2, hx)
-        pass_on(CHUNKS - 2 + hx // 2)
     for part in range(2):
         for hx in (part, part + 2):
             reduce_end(2, hx)
         key_send(part)
+    for j in range(CHUNKS - 4, CHUNKS):
+        pass_on(j)
     for j in range(CHUNKS):
         finish(j)
     for part in range(2):

time: 54.4 us -> 51.9 us (0.954)
  Pallas kernels: 52.2 us -> 49.7 us
    pallas_call x1, Pallas kernels: 52.2 us -> 49.7 us  [on_device(): pl.pallas_call(kernel, out_shape=(jax.ShapeDtypeStruct((groups, 16, width...]
where the time goes in v7:
time: 51.9 us; the launch traced here: 51.8 us
  Pallas kernels  49.7 us (96%)
  local copies, waits for them, and re-layouts  1.47 us (3%)
  between operations  0.64 us (1%)
    pallas_call x1, Pallas kernels, on_device(): pl.pallas_call(kernel, out_shape=(jax.ShapeDtypeStruct((groups, 16, width...  49.7 us
    unnamed x2, local copies, waits for them, and re-layouts  1.47 us

profile of v7, /device:TPU:1, one launch (start us, length us, event | category | flops | bytes accessed | tf_op | source)
XLA Modules:
  0.0 51.8 jit_solution(6584758629373204462)
XLA Ops:
  0.6 49.7 %shard_map.86 = (f32[4,16,256]{2,1,0:T(8,128)S(1)}, bf16[64,4096]{1,0:T(8,128)(2,1)S(1)}) custom-call(s32[4,32,256]{2,1,0:T(8,128)} %bitcast.10, s32[2,32,256]{2,1,0:T(8,128)} %bitcast.11, f32[2,32,256]{2,1,0:T(8,128)} %bitcast.12, f32[2,32,256]{2,1,0:T(8,128)} %bitcast.13, bf16[256,2,2,256]{3,2,1,0:T(2,128)(2,1)} %q_hbm.1, bf16[256,2,2,256]{3,2,1,0:T(2,128)(2,1)} %ks_hbm.1, ...), custom_call_target="tpu_custom_call" | custom-call | tf_op jit(solution)/shard_map/pallas_call | solution.py:323
  50.3 0.7 %copy.9 = f32[16,2,2,256]{3,2,1,0:T(2,128)} copy(f32[16,2,2,256]{3,0,2,1:T(8,128)S(1)} %bitcast.9) | data formatting | bytes 131072
  51.0 0.8 %copy.11 = bf16[64,4096]{1,0:T(8,128)(2,1)} copy(bf16[64,4096]{1,0:T(8,128)(2,1)S(1)} %get-tuple-element.11) | data formatting | bytes 1048576
